TPU v7x, 512 devices: a whole 4x4x16 slice. The times are simulated.
512 devices in a mesh: dp: 4 (over x), ep: 128 (over y, z, core).
Axes of the slice: x: 4, y: 4, z: 16, core: 2. Of those that a mesh axis runs over, the one named last changes fastest.
Arguments:
- hidden_states: bfloat16 [4096, 3584], P(('dp', 'ep')), parts along dimension 0, may hold values from -120 to 120
- norm_gain: float32 [3584], replicated, may hold values from 0.1 to 1.9
- expert_ids: int32 [4096, 8], P(('dp', 'ep')), parts along dimension 0, may hold values from 0 to 15, all different within a row; in each aligned block of 8 rows (0 to 7, 8 to 15, ...) at most 5 rows name the same one
- route_scores: float32 [4096, 8], P(('dp', 'ep')), parts along dimension 0, may hold values from 0.1 to 1
- gate_weight: bfloat16 [3584, 16384], P(None, 'ep'), may hold values from -0.09375 to 0.09375
- up_weight: bfloat16 [3584, 16384], P(None, 'ep'), may hold values from -0.09375 to 0.09375
- down_weight: bfloat16 [16384, 3584], P('ep'), may hold values from -0.1875 to 0.1875
- query_latent: bfloat16 [4096, 64, 512], P(('dp', 'ep')), parts along dimension 0, may hold values from -23 to 23
- query_rope: bfloat16 [4096, 4096], P(('dp', 'ep')), parts along dimension 0, may hold values from -23 to 23
- cache_latent: bfloat16 [512, 512, 512], P(('dp', 'ep')), parts along dimension 0, may hold values from -5.3 to 5.3
- cache_rope: bfloat16 [512, 64, 512], P(('dp', 'ep')), parts along dimension 0, may hold values from -5.3 to 5.3
- tree_latent: bfloat16 [4096, 512], P(('dp', 'ep')), parts along dimension 0, may hold values from -6 to 6
- tree_rope: bfloat16 [4096, 64], P(('dp', 'ep')), parts along dimension 0, may hold values from -6 to 6
- cache_lengths: int32 [512], P(('dp', 'ep')), parts along dimension 0, may hold values from 128 to 512, as said below
- tree_parents: int32 [4096], P(('dp', 'ep')), parts along dimension 0, may hold values from 0 to 6, as said below
Outputs:
- attention_out: bfloat16 [4096, 64, 512], P(('dp', 'ep')), parts along dimension 0
- expert_out: bfloat16 [4096, 3584], P(('dp', 'ep')), parts along dimension 0
There are 4 independent parts, one for each index of `dp`. A program takes and returns all parts, laid end to end along the dimension named above; an argument that names none is the same for every part. Nothing has to cross between parts.
Inputs may be any that keep to these rules, and one draw needn't show every extreme that they name: `expert_ids`: in the 8 rows of one device each expert is named by at most 5 rows, a bound that some block reaches; each row names 8 different experts. `cache_lengths`: some request holds exactly 512 positions. `tree_parents`: counting candidates from 0 within their request, candidate i > 0 has a parent below i, and candidate 0 has 0.
All inputs are finite; a program needn't handle non-finite values.
Results may differ from a plain program's by a relative error of at most 0.008.
Values may be sent and summed in bfloat16 or wider, within the bound.
No kernel may reach another device: no remote copies, remote signals or barrier semaphores. Data moves between devices by JAX's collectives and lax.ppermute only.
A program may use at most 64 MiB of HBM per device.

v0:
```python
import functools

import jax
import jax.numpy as jnp
from jax import lax
from jax.experimental import pallas as pl
from jax.experimental.pallas import tpu as pltpu
from jax.sharding import Mesh, PartitionSpec as P


EXPERTS = 16
MOST = 5
LANES = 128

softmax_scale = 192.0 ** (-0.5)
route_scale = 2.5
norm_eps = 1e-06
very_negative = -1e30
grid_axes = ("dp", "y", "z", "c")


def visible_tree(parents):
    tree_size = parents.shape[0]
    position = jnp.arange(tree_size, dtype=jnp.int32)
    parent_map = ((parents[:, None] == position[None, :]) & (position[:, None] > 0)).astype(
        jnp.float32
    )
    identity = jnp.eye(tree_size, dtype=jnp.float32)
    reached = identity
    for _ in range(tree_size):
        reached = jnp.minimum(
            identity + jnp.dot(parent_map, reached, precision=lax.Precision.HIGHEST), 1.0
        )
    return reached > 0.5


def attend_request(
    query_latent,
    query_rope,
    cache_latent,
    cache_rope,
    tree_latent,
    tree_rope,
    cache_length,
    parents,
):
    row_count = query_latent.shape[0]
    head_count = query_latent.shape[1]
    rope_width = tree_rope.shape[1]
    query_rotary = query_rope.reshape(row_count, head_count, rope_width)
    cache_scores = jnp.einsum(
        "rhc,lc->rhl", query_latent, cache_latent, preferred_element_type=jnp.float32
    )
    cache_scores = (
        cache_scores
        + jnp.einsum("rhc,cl->rhl", query_rotary, cache_rope, preferred_element_type=jnp.float32)
    ) * softmax_scale
    candidate_tree_scores = jnp.einsum(
        "rhc,jc->rhj", query_latent, tree_latent, preferred_element_type=jnp.float32
    )
    candidate_tree_scores = (
        candidate_tree_scores
        + jnp.einsum("rhc,jc->rhj", query_rotary, tree_rope, preferred_element_type=jnp.float32)
    ) * softmax_scale
    cache_live = (jnp.arange(cache_latent.shape[0], dtype=jnp.int32) < cache_length)[None, None, :]
    tree_seen = visible_tree(parents)[:, None, :]
    cache_scores = jnp.where(cache_live, cache_scores, very_negative)
    candidate_tree_scores = jnp.where(tree_seen, candidate_tree_scores, very_negative)
    row_peak = jnp.maximum(
        jnp.max(cache_scores, axis=-1, keepdims=True),
        jnp.max(candidate_tree_scores, axis=-1, keepdims=True),
    )
    cache_exp = jnp.where(cache_live, jnp.exp(cache_scores - row_peak), 0.0)
    tree_exp = jnp.where(tree_seen, jnp.exp(candidate_tree_scores - row_peak), 0.0)
    denominator = jnp.sum(cache_exp, axis=-1, keepdims=True) + jnp.sum(
        tree_exp, axis=-1, keepdims=True
    )
    cache_probs = (cache_exp / denominator).astype(jnp.bfloat16)
    tree_probs = (tree_exp / denominator).astype(jnp.bfloat16)
    attended = jnp.einsum(
        "rhl,lc->rhc", cache_probs, cache_latent, preferred_element_type=jnp.float32
    )
    attended = attended + jnp.einsum(
        "rhj,jc->rhc", tree_probs, tree_latent, preferred_element_type=jnp.float32
    )
    return attended.astype(jnp.bfloat16)


def pack_body(states, gain, ids, scores, out):
    value = states[...].astype(jnp.float32)
    row_count, width = value.shape
    mean = jnp.mean(value * value, axis=-1, keepdims=True)
    out[:, :width] = (value * lax.rsqrt(mean + norm_eps) * gain[...]).astype(jnp.bfloat16)
    score = scores[...]
    weight = (route_scale * score / jnp.sum(score, axis=-1, keepdims=True)).astype(jnp.bfloat16)
    weight = weight.astype(jnp.float32)
    names = ids[...]
    lane = lax.broadcasted_iota(jnp.int32, (row_count, LANES), 1)
    table = jnp.zeros((row_count, LANES), jnp.float32)
    for k in range(names.shape[1]):
        table += jnp.where(names[:, k : k + 1] == lane, weight[:, k : k + 1], 0.0)
    out[:, width:] = table.astype(jnp.bfloat16)


def select_body(row_count, gathered, *outs):
    chosen, weigh = outs[:-1], outs[-1]
    y_size = len(chosen)
    per_y = EXPERTS // y_size
    count = gathered.shape[0]
    width = gathered.shape[1] - LANES
    slots = chosen[0].shape[0]
    turn = lax.broadcasted_iota(jnp.int32, (8, LANES), 0)
    lane = lax.broadcasted_iota(jnp.int32, (8, LANES), 1)
    to = (lax.axis_index("y") + turn) % y_size
    expert = to * per_y + lax.axis_index("z") * per_y // lax.axis_size("z")
    column = jnp.where((lane == expert) & (turn < y_size), 1.0, 0.0).astype(jnp.bfloat16)
    share = lax.dot_general(
        column,
        gathered[:, width:],
        (((1,), (1,)), ((), ())),
        preferred_element_type=jnp.float32,
    )
    named = share > 0
    first = lax.broadcasted_iota(jnp.int32, (count, count), 0)
    second = lax.broadcasted_iota(jnp.int32, (count, count), 1)
    earlier = (first < second) & (first // row_count == second // row_count)
    slot = jnp.dot(
        jnp.where(named, 1.0, 0.0).astype(jnp.bfloat16),
        jnp.where(earlier, 1.0, 0.0).astype(jnp.bfloat16),
        preferred_element_type=jnp.float32,
    ).astype(jnp.int32)
    source = lax.broadcasted_iota(jnp.int32, (8, count), 1)
    target = jnp.where(named, source // row_count * MOST + slot, -1)
    place = lax.broadcasted_iota(jnp.int32, (slots, count), 0)
    for k in (2, 1, 3, 0):
        placed = place == target[k : k + 1, :]
        pick = jnp.where(placed, 1.0, 0.0).astype(jnp.bfloat16)
        chosen[k][...] = jnp.dot(
            pick, gathered[:, :width], preferred_element_type=jnp.float32
        ).astype(jnp.bfloat16)
        weigh[k] = jnp.where(placed, share[k : k + 1, :], 0.0).astype(jnp.bfloat16)


def shifted(value, axis, step):
    size = lax.axis_size(axis)
    return lax.ppermute(value, axis, [(i, (i + step) % size) for i in range(size)])


def expert_body(rows, gate_a, up_a, down_a, gate_b, up_b, down_b, out):
    value = rows[...]

    def hidden(gate, up):
        gate_act = jnp.dot(value, gate[...], preferred_element_type=jnp.float32)
        up_act = jnp.dot(value, up[...], preferred_element_type=jnp.float32)
        return (gate_act / (1.0 + jnp.exp(-gate_act)) * up_act).astype(jnp.bfloat16)

    total = jnp.dot(hidden(gate_a, up_a), down_a[...], preferred_element_type=jnp.float32)
    total += jnp.dot(hidden(gate_b, up_b), down_b[...], preferred_element_type=jnp.float32)
    out[...] = total.astype(jnp.bfloat16)


def expert_part(rows, weights):
    whole = pl.BlockSpec(memory_space=pltpu.VMEM)
    units = 2 * weights[0].shape[1]
    return pl.pallas_call(
        expert_body,
        out_shape=jax.ShapeDtypeStruct(rows.shape, jnp.bfloat16),
        in_specs=[whole] * 7,
        out_specs=whole,
        cost_estimate=pl.CostEstimate(
            flops=6 * rows.shape[0] * rows.shape[1] * units,
            transcendentals=rows.shape[0] * units,
            bytes_accessed=4 * rows.size + 6 * rows.shape[1] * units,
        ),
        compiler_params=pltpu.CompilerParams(vmem_limit_bytes=16 << 20),
    )(rows, *weights)


def layer(
    hidden_states,
    norm_gain,
    expert_ids,
    route_scores,
    gate_weight,
    up_weight,
    down_weight,
    query_latent,
    query_rope,
    cache_latent,
    cache_rope,
    tree_latent,
    tree_rope,
    cache_lengths,
    tree_parents,
):
    row_count, width = hidden_states.shape
    whole = pl.BlockSpec(memory_space=pltpu.VMEM)
    packed = pl.pallas_call(
        pack_body,
        out_shape=jax.ShapeDtypeStruct((row_count, width + LANES), jnp.bfloat16),
        in_specs=[whole] * 4,
        out_specs=whole,
    )(hidden_states, norm_gain[None, :], expert_ids, route_scores)
    gathered = lax.all_gather(packed, "z", axis=0, tiled=True)

    y_size = lax.axis_size("y")
    slots = gathered.shape[0] // row_count * MOST
    part = jax.ShapeDtypeStruct((slots, width), jnp.bfloat16)
    *chosen, weigh = pl.pallas_call(
        functools.partial(select_body, row_count),
        out_shape=[part] * y_size
        + [jax.ShapeDtypeStruct((y_size, slots, gathered.shape[0]), jnp.bfloat16)],
        in_specs=[whole],
        out_specs=[whole] * (y_size + 1),
    )(gathered)
    *chosen, gate_weight, up_weight, down_weight = lax.optimization_barrier(
        (*chosen, gate_weight, up_weight, down_weight)
    )
    own = (gate_weight, up_weight, down_weight)
    weights = own + tuple(shifted(w, "c", 1) for w in own)

    arrived = [chosen[0]]
    for k in range(1, y_size):
        arrived.append(shifted(chosen[k], "y", k))
    returned = []
    for k in range(y_size):
        answer = expert_part(arrived[k], weights)
        returned.append(shifted(answer, "y", -k) if k else answer)

    attention_out = attend_request(
        query_latent,
        query_rope,
        cache_latent[0],
        cache_rope[0],
        tree_latent,
        tree_rope,
        cache_lengths[0],
        tree_parents,
    )

    summed = sum(
        lax.dot_general(
            weigh[k], returned[k], (((0,), (0,)), ((), ())), preferred_element_type=jnp.float32
        )
        for k in range(y_size)
    ).astype(jnp.bfloat16)
    parts = lax.all_to_all(summed, "z", split_axis=0, concat_axis=0, tiled=True)
    expert_out = jnp.sum(parts.reshape(-1, row_count, width).astype(jnp.float32), axis=0)
    return (attention_out, expert_out.astype(jnp.bfloat16))


def solution(mesh):
    devices = mesh.devices.reshape(4, 4, 16, 2)
    grid = Mesh(devices, grid_axes)
    rows = P(grid_axes, None)
    ep = ("y", "z", "c")
    placed = (
        rows,
        P(),
        rows,
        rows,
        P(None, ep),
        P(None, ep),
        P(ep, None),
        P(grid_axes, None, None),
        rows,
        P(grid_axes, None, None),
        P(grid_axes, None, None),
        rows,
        rows,
        P(grid_axes),
        P(grid_axes),
    )
    return jax.shard_map(
        layer,
        mesh=grid,
        in_specs=placed,
        out_specs=(P(grid_axes, None, None), rows),
        check_vma=False,
    )
```

profile of v0, /device:TPU:46, one launch (start us, length us, event | category | flops | bytes accessed | tf_op | source)
XLA Modules:
  0.0 189.1 jit_solution(16956254334405001764)
XLA Ops:
  0.7 1.5 broadcast_in_dim.54.gain
  2.1 1.6 shard_map.158
  3.8 41.4 %all_gather.3.gathered = bf16[128,3712]{1,0:T(8,128)(2,1)} all-gather(bf16[8,3712]{1,0:T(8,128)(2,1)} %shard_map.158), channel_id=1, replica_groups=mesh['dp'=4,'y'=4,'z'=16,'c'=2] {'z'}, dimensions={0}, use_global_device_ids=true | all-gather | bytes 1009664 | tf_op jit(solution)/shard_map/all_gather | solution.py:204
  45.2 3.3 %shard_map.159 = (bf16[80,3584]{1,0:T(8,128)(2,1)}, bf16[80,3584]{1,0:T(8,128)(2,1)}, bf16[80,3584]{1,0:T(8,128)(2,1)}, bf16[80,3584]{1,0:T(8,128)(2,1)}, bf16[4,80,128]{2,1,0:T(8,128)(2,1)}) custom-call(bf16[128,3712]{1,0:T(8,128)(2,1)} %all_gather.3.gathered), custom_call_target="tpu_custom_call" | custom-call | tf_op jit(solution)/shard_map/pallas_call | solution.py:209
  48.6 1.9 %collective-permute-start = (bf16[3584,128]{1,0:T(8,128)(2,1)S(1)}, bf16[3584,128]{1,0:T(8,128)(2,1)S(1)}, u32[]{:S(2)}, u32[]{:S(2)}) collective-permute-start(bf16[3584,128]{1,0:T(8,128)(2,1)S(1)} %copy-done.1), channel_id=1, source_target_pairs={{0,1},{1,0},{2,3},{3,2},{4,5},{5,4},{6,7},{7,6},{8,9},{9,8},{10,11... | collective-permute-start | bytes 2752520 | tf_op jit(solution)/shard_map/ppermute | solution.py:146
  50.5 2.4 %collective-permute-start.1 = (bf16[3584,128]{1,0:T(8,128)(2,1)S(1)}, bf16[3584,128]{1,0:T(8,128)(2,1)S(1)}, u32[]{:S(2)}, u32[]{:S(2)}) collective-permute-start(bf16[3584,128]{1,0:T(8,128)(2,1)S(1)} %copy-done.2), channel_id=1, source_target_pairs={{0,1},{1,0},{2,3},{3,2},{4,5},{5,4},{6,7},{7,6},{8,9},{9,8},{10,11... | collective-permute-start | bytes 2752520 | tf_op jit(solution)/shard_map/ppermute | solution.py:146
  52.9 1.9 %collective-permute-start.2 = (bf16[128,3584]{1,0:T(8,128)(2,1)}, bf16[128,3584]{1,0:T(8,128)(2,1)S(1)}, u32[]{:S(2)}, u32[]{:S(2)}) collective-permute-start(bf16[128,3584]{1,0:T(8,128)(2,1)} %down_a.3), channel_id=1, source_target_pairs={{0,1},{1,0},{2,3},{3,2},{4,5},{5,4},{6,7},{7,6},{8,9},{9,8},{10,11... | collective-permute-start | bytes 2752520 | tf_op jit(solution)/shard_map/ppermute | solution.py:146
  54.8 2.4 %collective-permute-start.7 = (bf16[80,3584]{1,0:T(8,128)(2,1)}, bf16[80,3584]{1,0:T(8,128)(2,1)S(1)}, u32[]{:S(2)}, u32[]{:S(2)}) collective-permute-start(bf16[80,3584]{1,0:T(8,128)(2,1)} %get-tuple-element.25), channel_id=1, source_target_pairs={{0,96},{32,0},{64,32},{96,64},{1,97},{33,1},{65,33},{97,65},{2,98}... | collective-permute-start | bytes 1720328 | tf_op jit(solution)/shard_map/ppermute | solution.py:146
  57.2 4.5 %collective-permute-start.5 = (bf16[80,3584]{1,0:T(8,128)(2,1)}, bf16[80,3584]{1,0:T(8,128)(2,1)}, u32[]{:S(2)}, u32[]{:S(2)}) collective-permute-start(bf16[80,3584]{1,0:T(8,128)(2,1)} %get-tuple-element.24), channel_id=1, source_target_pairs={{0,64},{32,96},{64,0},{96,32},{1,65},{33,97},{65,1},{97,33},{2,66}... | collective-permute-start | bytes 1720328 | tf_op jit(solution)/shard_map/ppermute | solution.py:146
  61.7 10.6 %collective-permute-done.7.rows = bf16[80,3584]{1,0:T(8,128)(2,1)S(1)} collective-permute-done((bf16[80,3584]{1,0:T(8,128)(2,1)}, bf16[80,3584]{1,0:T(8,128)(2,1)S(1)}, u32[]{:S(2)}, u32[]{:S(2)}) %collective-permute-start.7) | collective-permute-done | bytes 573472 | tf_op jit(solution)/shard_map/ppermute | solution.py:146
  72.3 3.9 %collective-permute-start.3 = (bf16[80,3584]{1,0:T(8,128)(2,1)}, bf16[80,3584]{1,0:T(8,128)(2,1)}, u32[]{:S(2)}, u32[]{:S(2)}) collective-permute-start(bf16[80,3584]{1,0:T(8,128)(2,1)} %get-tuple-element.23), channel_id=1, source_target_pairs={{0,32},{32,64},{64,96},{96,0},{1,33},{33,65},{65,97},{97,1},{2,34}... | collective-permute-start | bytes 1720328 | tf_op jit(solution)/shard_map/ppermute | solution.py:146
  76.3 1.8 copy-done.3
  78.1 2.0 %shard_map.163 = bf16[80,3584]{1,0:T(8,128)(2,1)} custom-call(bf16[80,3584]{1,0:T(8,128)(2,1)S(1)} %collective-permute-done.7.rows, bf16[3584,128]{1,0:T(8,128)(2,1)S(1)} %copy-done.1, bf16[3584,128]{1,0:T(8,128)(2,1)S(1)} %copy-done.2, bf16[128,3584]{1,0:T(8,128)(2,1)S(1)} %copy-done.3, bf16[3584,128]{1,0:T(8,128)(2,1)S(1)} %collective-permute-done.gate_b, ...), custom_call_target="tpu_custom_call" | custom-call | flops 440401920 | bytes 6651904 | tf_op jit(solution)/shard_map/pallas_call | solution.py:165
  80.2 16.2 %collective-permute-start.8 = (bf16[80,3584]{1,0:T(8,128)(2,1)}, bf16[80,3584]{1,0:T(8,128)(2,1)}, u32[]{:S(2)}, u32[]{:S(2)}) collective-permute-start(bf16[80,3584]{1,0:T(8,128)(2,1)} %shard_map.163), channel_id=1, source_target_pairs={{0,32},{32,64},{64,96},{96,0},{1,33},{33,65},{65,97},{97,1},{2,34}... | collective-permute-start | bytes 1720328 | tf_op jit(solution)/shard_map/ppermute | solution.py:146
  97.1 0.2 reshape.34
  97.3 1.2 copy-done.6
  98.5 1.2 copy-done.9
  99.7 1.2 copy-done.12
  100.8 2.3 %shard_map.162 = bf16[80,3584]{1,0:T(8,128)(2,1)S(1)} custom-call(bf16[80,3584]{1,0:T(8,128)(2,1)} %collective-permute-done.5.rows, bf16[3584,128]{1,0:T(8,128)(2,1)S(1)} %copy-done.1, bf16[3584,128]{1,0:T(8,128)(2,1)S(1)} %copy-done.2, bf16[128,3584]{1,0:T(8,128)(2,1)S(1)} %copy-done.4, bf16[3584,128]{1,0:T(8,128)(2,1)S(1)} %copy-done.6, ...), custom_call_target="tpu_custom_call" | custom-call | flops 440401920 | bytes 6651904 | tf_op jit(solution)/shard_map/pallas_call | solution.py:165
  103.2 1.9 %collective-permute-start.6 = (bf16[80,3584]{1,0:T(8,128)(2,1)S(1)}, bf16[80,3584]{1,0:T(8,128)(2,1)S(1)}, u32[]{:S(2)}, u32[]{:S(2)}) collective-permute-start(bf16[80,3584]{1,0:T(8,128)(2,1)S(1)} %shard_map.162), channel_id=1, source_target_pairs={{0,64},{32,96},{64,0},{96,32},{1,65},{33,97},{65,1},{97,33},{2,66}... | collective-permute-start | bytes 1720328 | tf_op jit(solution)/shard_map/ppermute | solution.py:146
  105.1 0.2 fusion.16
  105.3 2.4 %shard_map.161 = bf16[80,3584]{1,0:T(8,128)(2,1)S(1)} custom-call(bf16[80,3584]{1,0:T(8,128)(2,1)} %collective-permute-done.3.rows, bf16[3584,128]{1,0:T(8,128)(2,1)S(1)} %copy-done.1, bf16[3584,128]{1,0:T(8,128)(2,1)S(1)} %copy-done.2, bf16[128,3584]{1,0:T(8,128)(2,1)S(1)} %copy-done.4, bf16[3584,128]{1,0:T(8,128)(2,1)S(1)} %copy-done.6, ...), custom_call_target="tpu_custom_call" | custom-call | flops 440401920 | bytes 6651904 | tf_op jit(solution)/shard_map/pallas_call | solution.py:165
  107.7 4.1 %collective-permute-start.4 = (bf16[80,3584]{1,0:T(8,128)(2,1)S(1)}, bf16[80,3584]{1,0:T(8,128)(2,1)S(1)}, u32[]{:S(2)}, u32[]{:S(2)}) collective-permute-start(bf16[80,3584]{1,0:T(8,128)(2,1)S(1)} %shard_map.161), channel_id=1, source_target_pairs={{0,96},{32,0},{64,32},{96,64},{1,97},{33,1},{65,33},{97,65},{2,98}... | collective-permute-start | bytes 1720328 | tf_op jit(solution)/shard_map/ppermute | solution.py:146
  111.8 1.2 shard_map.160
  113.1 1.0 collective-permute-done.8
  114.0 1.5 fusion.28
  115.5 7.0 %collective-permute-done.6 = bf16[80,3584]{1,0:T(8,128)(2,1)S(1)} collective-permute-done((bf16[80,3584]{1,0:T(8,128)(2,1)S(1)}, bf16[80,3584]{1,0:T(8,128)(2,1)S(1)}, u32[]{:S(2)}, u32[]{:S(2)}) %collective-permute-start.6) | collective-permute-done | bytes 573472 | tf_op jit(solution)/shard_map/ppermute | solution.py:146
  122.5 0.4 fusion.30
  122.9 9.9 %collective-permute-done.4 = bf16[80,3584]{1,0:T(8,128)(2,1)S(1)} collective-permute-done((bf16[80,3584]{1,0:T(8,128)(2,1)S(1)}, bf16[80,3584]{1,0:T(8,128)(2,1)S(1)}, u32[]{:S(2)}, u32[]{:S(2)}) %collective-permute-start.4) | collective-permute-done | bytes 573472 | tf_op jit(solution)/shard_map/ppermute | solution.py:146
  132.8 0.4 fusion.32
  133.2 1.4 fusion.3
  134.6 9.1 %all-to-all-start = ((bf16[16,8,3584]{2,1,0:T(8,128)(2,1)}), bf16[16,8,3584]{2,1,0:T(8,128)(2,1)S(1)}, u32[]{:S(2)}, u32[]{:S(2)}) async-start(bf16[16,8,3584]{2,1,0:T(8,128)(2,1)} %fusion.3), calls=%async_computation | async-start | bytes 1835008 | tf_op jit(solution)/shard_map/all_to_all | solution.py:247
  143.7 0.2 fusion.15
  143.9 0.2 fusion.14
  144.1 0.2 fusion.13
  144.3 0.2 fusion.12
  144.5 0.2 fusion.11
  144.7 0.2 fusion.10
  144.9 0.2 fusion.17
  145.1 0.3 fusion.44
  145.4 0.2 fusion.75
  145.7 0.5 fusion.21
  146.2 0.4 fusion.74
  146.6 0.3 fusion.18
  147.0 0.5 fusion.19
  147.5 1.2 fusion.6
  148.7 39.7 %all-to-all-done = bf16[16,8,3584]{2,1,0:T(8,128)(2,1)S(1)} async-done(((bf16[16,8,3584]{2,1,0:T(8,128)(2,1)}), bf16[16,8,3584]{2,1,0:T(8,128)(2,1)S(1)}, u32[]{:S(2)}, u32[]{:S(2)}) %all-to-all-start) | async-done | bytes 917536 | tf_op jit(solution)/shard_map/all_to_all | solution.py:247
  188.4 0.7 reduce_sum.32
  (48 shorter events, 0.2 us)
Async XLA Ops:
  0.6 145.0 %copy-start = (bf16[1,512,512]{2,1,0:T(8,128)(2,1)S(1)}, bf16[1,512,512]{2,1,0:T(8,128)(2,1)}, u32[]{:S(2)}) copy-start(bf16[1,512,512]{2,1,0:T(8,128)(2,1)} %param.24) | copy-start | bytes 1572868
  0.6 49.8 %copy-start.2 = (bf16[3584,128]{1,0:T(8,128)(2,1)S(1)}, bf16[3584,128]{1,0:T(8,128)(2,1)}, u32[]{:S(2)}) copy-start(bf16[3584,128]{1,0:T(8,128)(2,1)} %up_a.3) | copy-start | bytes 2752516
  0.7 47.9 %copy-start.1 = (bf16[3584,128]{1,0:T(8,128)(2,1)S(1)}, bf16[3584,128]{1,0:T(8,128)(2,1)}, u32[]{:S(2)}) copy-start(bf16[3584,128]{1,0:T(8,128)(2,1)} %gate_a.3) | copy-start | bytes 2752516
  45.2 51.8 %copy-start.16 = (bf16[8,4096]{1,0:T(8,128)(2,1)S(1)}, bf16[8,4096]{1,0:T(8,128)(2,1)}, u32[]{:S(2)}) copy-start(bf16[8,4096]{1,0:T(8,128)(2,1)} %param.23) | copy-start | bytes 196612
  48.6 27.7 %collective-permute-start = (bf16[3584,128]{1,0:T(8,128)(2,1)S(1)}, bf16[3584,128]{1,0:T(8,128)(2,1)S(1)}, u32[]{:S(2)}, u32[]{:S(2)}) collective-permute-start(bf16[3584,128]{1,0:T(8,128)(2,1)S(1)} %copy-done.1), channel_id=1, source_target_pairs={{0,1},{1,0},{2,3},{3,2},{4,5},{5,4},{6,7},{7,6},{8,9},{9,8},{10,11... | collective-permute-start | bytes 2752520 | tf_op jit(solution)/shard_map/ppermute | solution.py:146
  50.5 25.8 %collective-permute-start.1 = (bf16[3584,128]{1,0:T(8,128)(2,1)S(1)}, bf16[3584,128]{1,0:T(8,128)(2,1)S(1)}, u32[]{:S(2)}, u32[]{:S(2)}) collective-permute-start(bf16[3584,128]{1,0:T(8,128)(2,1)S(1)} %copy-done.2), channel_id=1, source_target_pairs={{0,1},{1,0},{2,3},{3,2},{4,5},{5,4},{6,7},{7,6},{8,9},{9,8},{10,11... | collective-permute-start | bytes 2752520 | tf_op jit(solution)/shard_map/ppermute | solution.py:146
  52.9 23.4 %collective-permute-start.2 = (bf16[128,3584]{1,0:T(8,128)(2,1)}, bf16[128,3584]{1,0:T(8,128)(2,1)S(1)}, u32[]{:S(2)}, u32[]{:S(2)}) collective-permute-start(bf16[128,3584]{1,0:T(8,128)(2,1)} %down_a.3), channel_id=1, source_target_pairs={{0,1},{1,0},{2,3},{3,2},{4,5},{5,4},{6,7},{7,6},{8,9},{9,8},{10,11... | collective-permute-start | bytes 2752520 | tf_op jit(solution)/shard_map/ppermute | solution.py:146
  54.8 17.5 %collective-permute-start.7 = (bf16[80,3584]{1,0:T(8,128)(2,1)}, bf16[80,3584]{1,0:T(8,128)(2,1)S(1)}, u32[]{:S(2)}, u32[]{:S(2)}) collective-permute-start(bf16[80,3584]{1,0:T(8,128)(2,1)} %get-tuple-element.25), channel_id=1, source_target_pairs={{0,96},{32,0},{64,32},{96,64},{1,97},{33,1},{65,33},{97,65},{2,98}... | collective-permute-start | bytes 1720328 | tf_op jit(solution)/shard_map/ppermute | solution.py:146
  57.2 40.1 %collective-permute-start.5 = (bf16[80,3584]{1,0:T(8,128)(2,1)}, bf16[80,3584]{1,0:T(8,128)(2,1)}, u32[]{:S(2)}, u32[]{:S(2)}) collective-permute-start(bf16[80,3584]{1,0:T(8,128)(2,1)} %get-tuple-element.24), channel_id=1, source_target_pairs={{0,64},{32,96},{64,0},{96,32},{1,65},{33,97},{65,1},{97,33},{2,66}... | collective-permute-start | bytes 1720328 | tf_op jit(solution)/shard_map/ppermute | solution.py:146
  72.3 33.0 %collective-permute-start.3 = (bf16[80,3584]{1,0:T(8,128)(2,1)}, bf16[80,3584]{1,0:T(8,128)(2,1)}, u32[]{:S(2)}, u32[]{:S(2)}) collective-permute-start(bf16[80,3584]{1,0:T(8,128)(2,1)} %get-tuple-element.23), channel_id=1, source_target_pairs={{0,32},{32,64},{64,96},{96,0},{1,33},{33,65},{65,97},{97,1},{2,34}... | collective-permute-start | bytes 1720328 | tf_op jit(solution)/shard_map/ppermute | solution.py:146
  76.3 3.9 %copy-start.5 = (bf16[3584,128]{1,0:T(8,128)(2,1)}, bf16[3584,128]{1,0:T(8,128)(2,1)S(1)}, u32[]{:S(2)}) copy-start(bf16[3584,128]{1,0:T(8,128)(2,1)S(1)} %collective-permute-done.gate_b) | copy-start | bytes 2752516
  76.3 3.9 %copy-start.8 = (bf16[3584,128]{1,0:T(8,128)(2,1)}, bf16[3584,128]{1,0:T(8,128)(2,1)S(1)}, u32[]{:S(2)}) copy-start(bf16[3584,128]{1,0:T(8,128)(2,1)S(1)} %collective-permute-done.1.up_b) | copy-start | bytes 2752516
  76.3 1.8 copy-start.3
  78.1 2.0 %copy-start.11 = (bf16[128,3584]{1,0:T(8,128)(2,1)}, bf16[128,3584]{1,0:T(8,128)(2,1)S(1)}, u32[]{:S(2)}) copy-start(bf16[128,3584]{1,0:T(8,128)(2,1)S(1)} %collective-permute-done.2.down_b) | copy-start | bytes 2752516
  78.1 19.1 %copy-start.4 = (bf16[128,3584]{1,0:T(8,128)(2,1)S(1)}, bf16[128,3584]{1,0:T(8,128)(2,1)}, u32[]{:S(2)}) copy-start(bf16[128,3584]{1,0:T(8,128)(2,1)} %down_a.3) | copy-start | bytes 2752516
  80.2 33.8 %collective-permute-start.8 = (bf16[80,3584]{1,0:T(8,128)(2,1)}, bf16[80,3584]{1,0:T(8,128)(2,1)}, u32[]{:S(2)}, u32[]{:S(2)}) collective-permute-start(bf16[80,3584]{1,0:T(8,128)(2,1)} %shard_map.163), channel_id=1, source_target_pairs={{0,32},{32,64},{64,96},{96,0},{1,33},{33,65},{65,97},{97,1},{2,34}... | collective-permute-start | bytes 1720328 | tf_op jit(solution)/shard_map/ppermute | solution.py:146
  97.3 1.2 copy-start.6
  98.5 1.2 copy-start.9
  99.7 1.2 copy-start.12
  100.8 4.3 %copy-start.20 = (s32[8]{0:T(128)S(1)}, s32[8]{0:T(128)}, u32[]{:S(2)}) copy-start(s32[8]{0:T(128)} %param.29) | copy-start | bytes 100
  100.8 4.5 %copy-start.10 = (bf16[3584,128]{1,0:T(8,128)(2,1)S(1)}, bf16[3584,128]{1,0:T(8,128)(2,1)}, u32[]{:S(2)}) copy-start(bf16[3584,128]{1,0:T(8,128)(2,1)} %copy-done.8) | copy-start | bytes 2752516
  103.2 19.3 %collective-permute-start.6 = (bf16[80,3584]{1,0:T(8,128)(2,1)S(1)}, bf16[80,3584]{1,0:T(8,128)(2,1)S(1)}, u32[]{:S(2)}, u32[]{:S(2)}) collective-permute-start(bf16[80,3584]{1,0:T(8,128)(2,1)S(1)} %shard_map.162), channel_id=1, source_target_pairs={{0,64},{32,96},{64,0},{96,32},{1,65},{33,97},{65,1},{97,33},{2,66}... | collective-permute-start | bytes 1720328 | tf_op jit(solution)/shard_map/ppermute | solution.py:146
  105.3 6.5 %copy-start.7 = (bf16[3584,128]{1,0:T(8,128)(2,1)S(1)}, bf16[3584,128]{1,0:T(8,128)(2,1)}, u32[]{:S(2)}) copy-start(bf16[3584,128]{1,0:T(8,128)(2,1)} %copy-done.5) | copy-start | bytes 2752516
  105.3 6.5 %copy-start.13 = (bf16[80,3584]{1,0:T(8,128)(2,1)S(1)}, bf16[80,3584]{1,0:T(8,128)(2,1)}, u32[]{:S(2)}) copy-start(bf16[80,3584]{1,0:T(8,128)(2,1)} %get-tuple-element.19.rows) | copy-start | bytes 1720324
  107.7 6.3 %copy-start.15 = (bf16[4,80,128]{2,1,0:T(8,128)(2,1)S(1)}, bf16[4,80,128]{2,1,0:T(8,128)(2,1)}, u32[]{:S(2)}) copy-start(bf16[4,80,128]{2,1,0:T(8,128)(2,1)} %get-tuple-element.14) | copy-start | bytes 245764
  107.7 25.1 %collective-permute-start.4 = (bf16[80,3584]{1,0:T(8,128)(2,1)S(1)}, bf16[80,3584]{1,0:T(8,128)(2,1)S(1)}, u32[]{:S(2)}, u32[]{:S(2)}) collective-permute-start(bf16[80,3584]{1,0:T(8,128)(2,1)S(1)} %shard_map.161), channel_id=1, source_target_pairs={{0,96},{32,0},{64,32},{96,64},{1,97},{33,1},{65,33},{97,65},{2,98}... | collective-permute-start | bytes 1720328 | tf_op jit(solution)/shard_map/ppermute | solution.py:146
  134.6 10.5 %copy-start.14 = (bf16[8,64,512]{2,1,0:T(8,128)(2,1)S(1)}, bf16[8,64,512]{2,1,0:T(8,128)(2,1)}, u32[]{:S(2)}) copy-start(bf16[8,64,512]{2,1,0:T(8,128)(2,1)} %param.22) | copy-start | bytes 1572868
  134.6 10.5 %copy-start.18 = (bf16[8,512]{1,0:T(8,128)(2,1)S(1)}, bf16[8,512]{1,0:T(8,128)(2,1)}, u32[]{:S(2)}) copy-start(bf16[8,512]{1,0:T(8,128)(2,1)} %param.26) | copy-start | bytes 24580
  134.6 10.8 %copy-start.19 = (bf16[8,64]{1,0:T(8,128)(2,1)S(1)}, bf16[8,64]{1,0:T(8,128)(2,1)}, u32[]{:S(2)}) copy-start(bf16[8,64]{1,0:T(8,128)(2,1)} %param.27) | copy-start | bytes 3076
  134.6 53.8 %all-to-all-start = ((bf16[16,8,3584]{2,1,0:T(8,128)(2,1)}), bf16[16,8,3584]{2,1,0:T(8,128)(2,1)S(1)}, u32[]{:S(2)}, u32[]{:S(2)}) async-start(bf16[16,8,3584]{2,1,0:T(8,128)(2,1)} %fusion.3), calls=%async_computation | async-start | bytes 1835008 | tf_op jit(solution)/shard_map/all_to_all | solution.py:247
  143.9 2.2 %copy-start.17 = (bf16[1,64,512]{2,1,0:T(8,128)(2,1)S(1)}, bf16[1,64,512]{2,1,0:T(8,128)(2,1)}, u32[]{:S(2)}) copy-start(bf16[1,64,512]{2,1,0:T(8,128)(2,1)} %param.25) | copy-start | bytes 196612
where the time goes:
time: 190 us; the launch traced here: 189 us
  waiting for transfers between devices  68.1 us (36%)
  starting transfers between devices  48.4 us (25%)
  blocking collectives  41.4 us (22%)
  Pallas kernels  12.9 us (7%)
  matrix products  8.36 us (4%)
  local copies, waits for them, and re-layouts  7.07 us (4%)
    all_gather x1, blocking collectives, layer(): gathered = lax.all_gather(packed, 'z', axis=0, tiled=True)  41.4 us
    all_to_all x1, waiting for transfers between devices, layer(): parts = lax.all_to_all(summed, 'z', split_axis=0, concat_axis=0, tiled=True)  39.7 us
    ppermute x9, starting transfers between devices, shifted(): lax.ppermute(value, axis, [(i, (i + step) % size) for i in range(size)])  39.3 us
    ppermute x9, waiting for transfers between devices, shifted(): lax.ppermute(value, axis, [(i, (i + step) % size) for i in range(size)])  28.5 us
    all_to_all x1, starting transfers between devices, layer(): parts = lax.all_to_all(summed, 'z', split_axis=0, concat_axis=0, tiled=True)  9.11 us
    pallas_call x4, Pallas kernels, expert_part(): pl.pallas_call(expert_body, out_shape=jax.ShapeDtypeStruct(rows.shape, jn...  7.96 us
    unnamed x42, local copies, waits for them, and re-layouts  5.42 us
  transfers between devices with their start and end apart: 10, of which 5 were waited for; matrix products, arithmetic and copies ran while one was open for 4% of the time, Pallas kernels for 4%

commit v1 on v0

--- a/solution.py
+++ b/solution.py
@@ -146,8 +146,13 @@
     return lax.ppermute(value, axis, [(i, (i + step) % size) for i in range(size)])
 
 
-def expert_body(rows, gate_a, up_a, down_a, gate_b, up_b, down_b, out):
-    value = rows[...]
+def expert_body(count, *refs):
+    rows, (gate_a, up_a, down_a, gate_b, up_b, down_b), outs = (
+        refs[:count],
+        refs[count : count + 6],
+        refs[count + 6 :],
+    )
+    value = jnp.concatenate([row[...] for row in rows], axis=0)
 
     def hidden(gate, up):
         gate_act = jnp.dot(value, gate[...], preferred_element_type=jnp.float32)
@@ -156,24 +161,40 @@
 
     total = jnp.dot(hidden(gate_a, up_a), down_a[...], preferred_element_type=jnp.float32)
     total += jnp.dot(hidden(gate_b, up_b), down_b[...], preferred_element_type=jnp.float32)
-    out[...] = total.astype(jnp.bfloat16)
+    size = rows[0].shape[0]
+    for k, out in enumerate(outs):
+        out[...] = total[k * size : (k + 1) * size].astype(jnp.bfloat16)
 
 
 def expert_part(rows, weights):
     whole = pl.BlockSpec(memory_space=pltpu.VMEM)
     units = 2 * weights[0].shape[1]
+    size, width = len(rows) * rows[0].shape[0], rows[0].shape[1]
     return pl.pallas_call(
-        expert_body,
-        out_shape=jax.ShapeDtypeStruct(rows.shape, jnp.bfloat16),
-        in_specs=[whole] * 7,
-        out_specs=whole,
+        functools.partial(expert_body, len(rows)),
+        out_shape=[jax.ShapeDtypeStruct(row.shape, jnp.bfloat16) for row in rows],
+        in_specs=[whole] * (len(rows) + 6),
+        out_specs=[whole] * len(rows),
         cost_estimate=pl.CostEstimate(
-            flops=6 * rows.shape[0] * rows.shape[1] * units,
-            transcendentals=rows.shape[0] * units,
-            bytes_accessed=4 * rows.size + 6 * rows.shape[1] * units,
+            flops=6 * size * width * units,
+            transcendentals=size * units,
+            bytes_accessed=4 * size * width + 6 * width * units,
         ),
-        compiler_params=pltpu.CompilerParams(vmem_limit_bytes=16 << 20),
-    )(rows, *weights)
+        compiler_params=pltpu.CompilerParams(vmem_limit_bytes=28 << 20),
+    )(*rows, *weights)
+
+
+def expand_body(weigh, *refs):
+    out = refs[-1]
+    total = jnp.zeros(out.shape, jnp.float32)
+    for k, answer in enumerate(refs[:-1]):
+        total += lax.dot_general(
+            weigh[k],
+            answer[...],
+            (((0,), (0,)), ((), ())),
+            preferred_element_type=jnp.float32,
+        )
+    out[...] = total.astype(jnp.bfloat16)
 
 
 def layer(
@@ -200,7 +221,7 @@
         out_shape=jax.ShapeDtypeStruct((row_count, width + LANES), jnp.bfloat16),
         in_specs=[whole] * 4,
         out_specs=whole,
-    )(hidden_states, norm_gain[None, :], expert_ids, route_scores)
+    )(hidden_states, norm_gain, expert_ids, route_scores)
     gathered = lax.all_gather(packed, "z", axis=0, tiled=True)
 
     y_size = lax.axis_size("y")
@@ -212,6 +233,7 @@
         + [jax.ShapeDtypeStruct((y_size, slots, gathered.shape[0]), jnp.bfloat16)],
         in_specs=[whole],
         out_specs=[whole] * (y_size + 1),
+        compiler_params=pltpu.CompilerParams(vmem_limit_bytes=16 << 20),
     )(gathered)
     *chosen, gate_weight, up_weight, down_weight = lax.optimization_barrier(
         (*chosen, gate_weight, up_weight, down_weight)
@@ -222,10 +244,10 @@
     arrived = [chosen[0]]
     for k in range(1, y_size):
         arrived.append(shifted(chosen[k], "y", k))
-    returned = []
-    for k in range(y_size):
-        answer = expert_part(arrived[k], weights)
-        returned.append(shifted(answer, "y", -k) if k else answer)
+    answers = expert_part(arrived, weights)
+    returned = [answers[0]]
+    for k in range(1, y_size):
+        returned.append(shifted(answers[k], "y", -k))
 
     attention_out = attend_request(
         query_latent,
@@ -238,12 +260,13 @@
         tree_parents,
     )
 
-    summed = sum(
-        lax.dot_general(
-            weigh[k], returned[k], (((0,), (0,)), ((), ())), preferred_element_type=jnp.float32
-        )
-        for k in range(y_size)
-    ).astype(jnp.bfloat16)
+    summed = pl.pallas_call(
+        expand_body,
+        out_shape=jax.ShapeDtypeStruct((gathered.shape[0], width), jnp.bfloat16),
+        in_specs=[whole] * (y_size + 1),
+        out_specs=whole,
+        compiler_params=pltpu.CompilerParams(vmem_limit_bytes=16 << 20),
+    )(weigh, *returned)
     parts = lax.all_to_all(summed, "z", split_axis=0, concat_axis=0, tiled=True)
     expert_out = jnp.sum(parts.reshape(-1, row_count, width).astype(jnp.float32), axis=0)
     return (attention_out, expert_out.astype(jnp.bfloat16))

time: 190 us -> 180 us (0.947)
  the two profiles are of different devices: /device:TPU:46 before, /device:TPU:38 now
where the time goes in v1:
time: 180 us
  waiting for transfers between devices  82.6 us (46%)
  blocking collectives  39.1 us (22%)
  starting transfers between devices  37 us (21%)
  Pallas kernels  9.55 us (5%)
  matrix products  4.64 us (3%)
  local copies, waits for them, and re-layouts  4.16 us (2%)
    ppermute x9, waiting for transfers between devices, shifted(): lax.ppermute(value, axis, [(i, (i + step) % size) for i in range(size)])  44.4 us
    all_gather x1, blocking collectives, layer(): gathered = lax.all_gather(packed, 'z', axis=0, tiled=True)  39.1 us
    all_to_all x1, waiting for transfers between devices, layer(): parts = lax.all_to_all(summed, 'z', split_axis=0, concat_axis=0, tiled=True)  38.2 us
    ppermute x9, starting transfers between devices, shifted(): lax.ppermute(value, axis, [(i, (i + step) % size) for i in range(size)])  28.1 us
    all_to_all x1, starting transfers between devices, layer(): parts = lax.all_to_all(summed, 'z', split_axis=0, concat_axis=0, tiled=True)  8.83 us
    pallas_call x1, Pallas kernels, expert_part(): pl.pallas_call(functools.partial(expert_body, len(rows)), out_shape=[jax....  4.78 us
  transfers between devices with their start and end apart: 10, of which 5 were waited for; matrix products, arithmetic and copies ran while one was open for 3% of the time, Pallas kernels for 0%

profile of v1, /device:TPU:38, one launch (start us, length us, event | category | flops | bytes accessed | tf_op | source)
XLA Modules:
  0.0 179.8 jit_solution(3372587590628341502)
XLA Ops:
  0.6 0.0 copy-start
  0.6 1.7 shard_map.158
  2.4 39.1 %all_gather.3.gathered = bf16[128,3712]{1,0:T(8,128)(2,1)S(1)} all-gather(bf16[8,3712]{1,0:T(8,128)(2,1)} %shard_map.158), channel_id=1, replica_groups=mesh['dp'=4,'y'=4,'z'=16,'c'=2] {'z'}, dimensions={0}, use_global_device_ids=true | all-gather | bytes 1009664 | tf_op jit(solution)/shard_map/all_gather | solution.py:225
  41.5 1.0 shard_map.159
  42.5 3.5 %collective-permute-start = (bf16[80,3584]{1,0:T(8,128)(2,1)S(1)}, bf16[80,3584]{1,0:T(8,128)(2,1)S(1)}, u32[]{:S(2)}, u32[]{:S(2)}) collective-permute-start(bf16[80,3584]{1,0:T(8,128)(2,1)S(1)} %get-tuple-element.24), channel_id=1, source_target_pairs={{0,32},{32,64},{64,96},{96,0},{1,33},{33,65},{65,97},{97,1},{2,34}... | collective-permute-start | bytes 1720328 | tf_op jit(solution)/shard_map/ppermute | solution.py:146
  46.0 1.9 %collective-permute-start.3 = (bf16[3584,128]{1,0:T(8,128)(2,1)S(1)}, bf16[3584,128]{1,0:T(8,128)(2,1)S(1)}, u32[]{:S(2)}, u32[]{:S(2)}) collective-permute-start(bf16[3584,128]{1,0:T(8,128)(2,1)S(1)} %copy-done.1), channel_id=1, source_target_pairs={{0,1},{1,0},{2,3},{3,2},{4,5},{5,4},{6,7},{7,6},{8,9},{9,8},{10,11... | collective-permute-start | bytes 2752520 | tf_op jit(solution)/shard_map/ppermute | solution.py:146
  48.0 2.4 %collective-permute-start.4 = (bf16[3584,128]{1,0:T(8,128)(2,1)S(1)}, bf16[3584,128]{1,0:T(8,128)(2,1)S(1)}, u32[]{:S(2)}, u32[]{:S(2)}) collective-permute-start(bf16[3584,128]{1,0:T(8,128)(2,1)S(1)} %copy-done.2), channel_id=1, source_target_pairs={{0,1},{1,0},{2,3},{3,2},{4,5},{5,4},{6,7},{7,6},{8,9},{9,8},{10,11... | collective-permute-start | bytes 2752520 | tf_op jit(solution)/shard_map/ppermute | solution.py:146
  50.4 1.9 %collective-permute-start.5 = (bf16[128,3584]{1,0:T(8,128)(2,1)}, bf16[128,3584]{1,0:T(8,128)(2,1)S(1)}, u32[]{:S(2)}, u32[]{:S(2)}) collective-permute-start(bf16[128,3584]{1,0:T(8,128)(2,1)} %refs_6_), channel_id=1, source_target_pairs={{0,1},{1,0},{2,3},{3,2},{4,5},{5,4},{6,7},{7,6},{8,9},{9,8},{10,11... | collective-permute-start | bytes 2752520 | tf_op jit(solution)/shard_map/ppermute | solution.py:146
  52.3 4.8 %collective-permute-start.1 = (bf16[80,3584]{1,0:T(8,128)(2,1)S(1)}, bf16[80,3584]{1,0:T(8,128)(2,1)S(1)}, u32[]{:S(2)}, u32[]{:S(2)}) collective-permute-start(bf16[80,3584]{1,0:T(8,128)(2,1)S(1)} %get-tuple-element.25), channel_id=1, source_target_pairs={{0,64},{32,96},{64,0},{96,32},{1,65},{33,97},{65,1},{97,33},{2,66}... | collective-permute-start | bytes 1720328 | tf_op jit(solution)/shard_map/ppermute | solution.py:146
  57.1 0.0 collective-permute-done.refs_1_
  57.1 3.3 %collective-permute-start.2 = (bf16[80,3584]{1,0:T(8,128)(2,1)S(1)}, bf16[80,3584]{1,0:T(8,128)(2,1)S(1)}, u32[]{:S(2)}, u32[]{:S(2)}) collective-permute-start(bf16[80,3584]{1,0:T(8,128)(2,1)S(1)} %get-tuple-element.26), channel_id=1, source_target_pairs={{0,96},{32,0},{64,32},{96,64},{1,97},{33,1},{65,33},{97,65},{2,98}... | collective-permute-start | bytes 1720328 | tf_op jit(solution)/shard_map/ppermute | solution.py:146
  60.4 10.7 %collective-permute-done.1.refs_2_ = bf16[80,3584]{1,0:T(8,128)(2,1)S(1)} collective-permute-done((bf16[80,3584]{1,0:T(8,128)(2,1)S(1)}, bf16[80,3584]{1,0:T(8,128)(2,1)S(1)}, u32[]{:S(2)}, u32[]{:S(2)}) %collective-permute-start.1) | collective-permute-done | bytes 573472 | tf_op jit(solution)/shard_map/ppermute | solution.py:146
  71.1 11.3 %collective-permute-done.2.refs_3_ = bf16[80,3584]{1,0:T(8,128)(2,1)S(1)} collective-permute-done((bf16[80,3584]{1,0:T(8,128)(2,1)S(1)}, bf16[80,3584]{1,0:T(8,128)(2,1)S(1)}, u32[]{:S(2)}, u32[]{:S(2)}) %collective-permute-start.2) | collective-permute-done | bytes 573472 | tf_op jit(solution)/shard_map/ppermute | solution.py:146
  82.4 0.0 copy-start.3
  82.4 1.2 copy-done.3
  83.6 4.8 %shard_map.160 = (bf16[80,3584]{1,0:T(8,128)(2,1)S(1)}, bf16[80,3584]{1,0:T(8,128)(2,1)}, bf16[80,3584]{1,0:T(8,128)(2,1)}, bf16[80,3584]{1,0:T(8,128)(2,1)S(1)}) custom-call(bf16[80,3584]{1,0:T(8,128)(2,1)S(1)} %get-tuple-element.23.refs_0_, bf16[80,3584]{1,0:T(8,128)(2,1)S(1)} %collective-permute-done.refs_1_, ...), custom_call_target="tpu_custom_call" | custom-call | flops 1761607680 | bytes 10092544 | tf_op jit(solution)/shard_map/pallas_call | solution.py:173
  88.4 4.5 %collective-permute-start.6 = (bf16[80,3584]{1,0:T(8,128)(2,1)}, bf16[80,3584]{1,0:T(8,128)(2,1)S(1)}, u32[]{:S(2)}, u32[]{:S(2)}) collective-permute-start(bf16[80,3584]{1,0:T(8,128)(2,1)} %get-tuple-element.31), channel_id=1, source_target_pairs={{0,96},{32,0},{64,32},{96,64},{1,97},{33,1},{65,33},{97,65},{2,98}... | collective-permute-start | bytes 1720328 | tf_op jit(solution)/shard_map/ppermute | solution.py:146
  92.9 3.9 %collective-permute-start.7 = (bf16[80,3584]{1,0:T(8,128)(2,1)}, bf16[80,3584]{1,0:T(8,128)(2,1)S(1)}, u32[]{:S(2)}, u32[]{:S(2)}) collective-permute-start(bf16[80,3584]{1,0:T(8,128)(2,1)} %get-tuple-element.32), channel_id=1, source_target_pairs={{0,64},{32,96},{64,0},{96,32},{1,65},{33,97},{65,1},{97,33},{2,66}... | collective-permute-start | bytes 1720328 | tf_op jit(solution)/shard_map/ppermute | solution.py:146
  96.8 1.9 %collective-permute-start.8 = (bf16[80,3584]{1,0:T(8,128)(2,1)S(1)}, bf16[80,3584]{1,0:T(8,128)(2,1)S(1)}, u32[]{:S(2)}, u32[]{:S(2)}) collective-permute-start(bf16[80,3584]{1,0:T(8,128)(2,1)S(1)} %get-tuple-element.33), channel_id=1, source_target_pairs={{0,32},{32,64},{64,96},{96,0},{1,33},{33,65},{65,97},{97,1},{2,34}... | collective-permute-start | bytes 1720328 | tf_op jit(solution)/shard_map/ppermute | solution.py:146
  98.7 0.8 reshape.34
  100.3 0.0 copy-start.10
  100.3 0.6 copy-done.10
  100.9 0.2 fusion.12
  101.1 16.9 %collective-permute-done.6.refs_1_ = bf16[80,3584]{1,0:T(8,128)(2,1)S(1)} collective-permute-done((bf16[80,3584]{1,0:T(8,128)(2,1)}, bf16[80,3584]{1,0:T(8,128)(2,1)S(1)}, u32[]{:S(2)}, u32[]{:S(2)}) %collective-permute-start.6) | collective-permute-done | bytes 573472 | tf_op jit(solution)/shard_map/ppermute | solution.py:146
  118.0 5.5 %collective-permute-done.8.refs_3_ = bf16[80,3584]{1,0:T(8,128)(2,1)S(1)} collective-permute-done((bf16[80,3584]{1,0:T(8,128)(2,1)S(1)}, bf16[80,3584]{1,0:T(8,128)(2,1)S(1)}, u32[]{:S(2)}, u32[]{:S(2)}) %collective-permute-start.8) | collective-permute-done | bytes 573472 | tf_op jit(solution)/shard_map/ppermute | solution.py:146
  123.5 2.1 %shard_map.161 = bf16[128,3584]{1,0:T(8,128)(2,1)} custom-call(bf16[4,80,128]{2,1,0:T(8,128)(2,1)S(1)} %get-tuple-element.18.weigh, bf16[80,3584]{1,0:T(8,128)(2,1)S(1)} %get-tuple-element.30.refs_0_, bf16[80,3584]{1,0:T(8,128)(2,1)S(1)} %collective-permute-done.6.refs_1_, bf16[80,3584]{1,0:T(8,128)(2,1)S(1)} %collective-permute-done.7.refs_2_, ...), custom_call_target="tpu_custom_call" | custom-call | tf_op jit(solution)/shard_map/pallas_call | solution.py:263
  125.5 8.8 %all-to-all-start = ((bf16[16,8,3584]{2,1,0:T(8,128)(2,1)}), bf16[16,8,3584]{2,1,0:T(8,128)(2,1)S(1)}, u32[]{:S(2)}, u32[]{:S(2)}) async-start(bf16[16,8,3584]{2,1,0:T(8,128)(2,1)} %bitcast.7), calls=%async_computation | async-start | bytes 1835008 | tf_op jit(solution)/shard_map/all_to_all | solution.py:270
  134.4 0.2 fusion.11
  134.5 0.2 fusion.10
  134.7 0.2 fusion.9
  134.9 0.2 fusion.8
  135.1 0.2 fusion.7
  135.3 0.2 fusion.6
  135.5 0.2 fusion.13
  135.7 0.5 copy-done.8
  136.2 0.3 fusion.29
  136.5 0.6 copy-done.5
  137.2 0.2 fusion.60
  137.4 0.0 copy-start.7
  137.4 0.5 fusion.17
  137.9 0.4 copy-done.7
  138.2 0.4 fusion.59
  138.6 0.1 fusion.23
  138.7 0.3 fusion.14
  139.1 0.5 fusion.15
  139.6 1.2 fusion.2
  140.8 38.2 %all-to-all-done = bf16[16,8,3584]{2,1,0:T(8,128)(2,1)S(1)} async-done(((bf16[16,8,3584]{2,1,0:T(8,128)(2,1)}), bf16[16,8,3584]{2,1,0:T(8,128)(2,1)S(1)}, u32[]{:S(2)}, u32[]{:S(2)}) %all-to-all-start) | async-done | bytes 917536 | tf_op jit(solution)/shard_map/all_to_all | solution.py:270
  179.0 0.7 reduce_sum.32
  (21 shorter events, 0.1 us)
Async XLA Ops:
  0.6 136.8 %copy-start = (bf16[1,512,512]{2,1,0:T(8,128)(2,1)S(1)}, bf16[1,512,512]{2,1,0:T(8,128)(2,1)}, u32[]{:S(2)}) copy-start(bf16[1,512,512]{2,1,0:T(8,128)(2,1)} %param.24) | copy-start | bytes 1572868
  2.4 43.7 %copy-start.1 = (bf16[3584,128]{1,0:T(8,128)(2,1)S(1)}, bf16[3584,128]{1,0:T(8,128)(2,1)}, u32[]{:S(2)}) copy-start(bf16[3584,128]{1,0:T(8,128)(2,1)} %refs_4_) | copy-start | bytes 2752516
  2.4 45.6 %copy-start.2 = (bf16[3584,128]{1,0:T(8,128)(2,1)S(1)}, bf16[3584,128]{1,0:T(8,128)(2,1)}, u32[]{:S(2)}) copy-start(bf16[3584,128]{1,0:T(8,128)(2,1)} %refs_5_) | copy-start | bytes 2752516
  41.5 57.2 %copy-start.6 = (bf16[8,4096]{1,0:T(8,128)(2,1)S(1)}, bf16[8,4096]{1,0:T(8,128)(2,1)}, u32[]{:S(2)}) copy-start(bf16[8,4096]{1,0:T(8,128)(2,1)} %param.23) | copy-start | bytes 196612
  42.5 14.6 %collective-permute-start = (bf16[80,3584]{1,0:T(8,128)(2,1)S(1)}, bf16[80,3584]{1,0:T(8,128)(2,1)S(1)}, u32[]{:S(2)}, u32[]{:S(2)}) collective-permute-start(bf16[80,3584]{1,0:T(8,128)(2,1)S(1)} %get-tuple-element.24), channel_id=1, source_target_pairs={{0,32},{32,64},{64,96},{96,0},{1,33},{33,65},{65,97},{97,1},{2,34}... | collective-permute-start | bytes 1720328 | tf_op jit(solution)/shard_map/ppermute | solution.py:146
  46.0 36.4 %collective-permute-start.3 = (bf16[3584,128]{1,0:T(8,128)(2,1)S(1)}, bf16[3584,128]{1,0:T(8,128)(2,1)S(1)}, u32[]{:S(2)}, u32[]{:S(2)}) collective-permute-start(bf16[3584,128]{1,0:T(8,128)(2,1)S(1)} %copy-done.1), channel_id=1, source_target_pairs={{0,1},{1,0},{2,3},{3,2},{4,5},{5,4},{6,7},{7,6},{8,9},{9,8},{10,11... | collective-permute-start | bytes 2752520 | tf_op jit(solution)/shard_map/ppermute | solution.py:146
  48.0 34.4 %collective-permute-start.4 = (bf16[3584,128]{1,0:T(8,128)(2,1)S(1)}, bf16[3584,128]{1,0:T(8,128)(2,1)S(1)}, u32[]{:S(2)}, u32[]{:S(2)}) collective-permute-start(bf16[3584,128]{1,0:T(8,128)(2,1)S(1)} %copy-done.2), channel_id=1, source_target_pairs={{0,1},{1,0},{2,3},{3,2},{4,5},{5,4},{6,7},{7,6},{8,9},{9,8},{10,11... | collective-permute-start | bytes 2752520 | tf_op jit(solution)/shard_map/ppermute | solution.py:146
  50.4 32.0 %collective-permute-start.5 = (bf16[128,3584]{1,0:T(8,128)(2,1)}, bf16[128,3584]{1,0:T(8,128)(2,1)S(1)}, u32[]{:S(2)}, u32[]{:S(2)}) collective-permute-start(bf16[128,3584]{1,0:T(8,128)(2,1)} %refs_6_), channel_id=1, source_target_pairs={{0,1},{1,0},{2,3},{3,2},{4,5},{5,4},{6,7},{7,6},{8,9},{9,8},{10,11... | collective-permute-start | bytes 2752520 | tf_op jit(solution)/shard_map/ppermute | solution.py:146
  52.3 18.8 %collective-permute-start.1 = (bf16[80,3584]{1,0:T(8,128)(2,1)S(1)}, bf16[80,3584]{1,0:T(8,128)(2,1)S(1)}, u32[]{:S(2)}, u32[]{:S(2)}) collective-permute-start(bf16[80,3584]{1,0:T(8,128)(2,1)S(1)} %get-tuple-element.25), channel_id=1, source_target_pairs={{0,64},{32,96},{64,0},{96,32},{1,65},{33,97},{65,1},{97,33},{2,66}... | collective-permute-start | bytes 1720328 | tf_op jit(solution)/shard_map/ppermute | solution.py:146
  57.1 25.3 %collective-permute-start.2 = (bf16[80,3584]{1,0:T(8,128)(2,1)S(1)}, bf16[80,3584]{1,0:T(8,128)(2,1)S(1)}, u32[]{:S(2)}, u32[]{:S(2)}) collective-permute-start(bf16[80,3584]{1,0:T(8,128)(2,1)S(1)} %get-tuple-element.26), channel_id=1, source_target_pairs={{0,96},{32,0},{64,32},{96,64},{1,97},{33,1},{65,33},{97,65},{2,98}... | collective-permute-start | bytes 1720328 | tf_op jit(solution)/shard_map/ppermute | solution.py:146
  82.4 1.2 copy-start.3
  88.4 29.6 %collective-permute-start.6 = (bf16[80,3584]{1,0:T(8,128)(2,1)}, bf16[80,3584]{1,0:T(8,128)(2,1)S(1)}, u32[]{:S(2)}, u32[]{:S(2)}) collective-permute-start(bf16[80,3584]{1,0:T(8,128)(2,1)} %get-tuple-element.31), channel_id=1, source_target_pairs={{0,96},{32,0},{64,32},{96,64},{1,97},{33,1},{65,33},{97,65},{2,98}... | collective-permute-start | bytes 1720328 | tf_op jit(solution)/shard_map/ppermute | solution.py:146
  92.9 25.1 %collective-permute-start.7 = (bf16[80,3584]{1,0:T(8,128)(2,1)}, bf16[80,3584]{1,0:T(8,128)(2,1)S(1)}, u32[]{:S(2)}, u32[]{:S(2)}) collective-permute-start(bf16[80,3584]{1,0:T(8,128)(2,1)} %get-tuple-element.32), channel_id=1, source_target_pairs={{0,64},{32,96},{64,0},{96,32},{1,65},{33,97},{65,1},{97,33},{2,66}... | collective-permute-start | bytes 1720328 | tf_op jit(solution)/shard_map/ppermute | solution.py:146
  96.8 26.6 %collective-permute-start.8 = (bf16[80,3584]{1,0:T(8,128)(2,1)S(1)}, bf16[80,3584]{1,0:T(8,128)(2,1)S(1)}, u32[]{:S(2)}, u32[]{:S(2)}) collective-permute-start(bf16[80,3584]{1,0:T(8,128)(2,1)S(1)} %get-tuple-element.33), channel_id=1, source_target_pairs={{0,32},{32,64},{64,96},{96,0},{1,33},{33,65},{65,97},{97,1},{2,34}... | collective-permute-start | bytes 1720328 | tf_op jit(solution)/shard_map/ppermute | solution.py:146
  100.3 0.7 copy-start.10
  125.5 53.5 %all-to-all-start = ((bf16[16,8,3584]{2,1,0:T(8,128)(2,1)}), bf16[16,8,3584]{2,1,0:T(8,128)(2,1)S(1)}, u32[]{:S(2)}, u32[]{:S(2)}) async-start(bf16[16,8,3584]{2,1,0:T(8,128)(2,1)} %bitcast.7), calls=%async_computation | async-start | bytes 1835008 | tf_op jit(solution)/shard_map/all_to_all | solution.py:270
  134.4 1.4 copy-start.4
  135.5 0.7 copy-start.8
  136.2 0.9 copy-start.5
  136.2 0.9 copy-start.9
  137.4 0.8 copy-start.7

commit v2 on v1

--- a/solution.py
+++ b/solution.py
@@ -16,7 +16,8 @@
 route_scale = 2.5
 norm_eps = 1e-06
 very_negative = -1e30
-grid_axes = ("dp", "y", "z", "c")
+grid_axes = ("dp", "y", "zi", "zp", "c")
+z_axes = ("zi", "zp")
 
 
 def visible_tree(parents):
@@ -112,7 +113,7 @@
     turn = lax.broadcasted_iota(jnp.int32, (8, LANES), 0)
     lane = lax.broadcasted_iota(jnp.int32, (8, LANES), 1)
     to = (lax.axis_index("y") + turn) % y_size
-    expert = to * per_y + lax.axis_index("z") * per_y // lax.axis_size("z")
+    expert = to * per_y + z_index() * per_y // z_size()
     column = jnp.where((lane == expert) & (turn < y_size), 1.0, 0.0).astype(jnp.bfloat16)
     share = lax.dot_general(
         column,
@@ -141,8 +142,16 @@
         weigh[k] = jnp.where(placed, share[k : k + 1, :], 0.0).astype(jnp.bfloat16)
 
 
+def z_index():
+    return lax.axis_index("zi") * lax.axis_size("zp") + lax.axis_index("zp")
+
+
+def z_size():
+    return lax.axis_size("zi") * lax.axis_size("zp")
+
+
 def shifted(value, axis, step):
-    size = lax.axis_size(axis)
+    size = z_size() if axis == z_axes else lax.axis_size(axis)
     return lax.ppermute(value, axis, [(i, (i + step) % size) for i in range(size)])
 
 
@@ -184,17 +193,42 @@
     )(*rows, *weights)
 
 
-def expand_body(weigh, *refs):
-    out = refs[-1]
-    total = jnp.zeros(out.shape, jnp.float32)
-    for k, answer in enumerate(refs[:-1]):
+def expand_body(row_count, weigh, *refs):
+    answers, (keep, left, right, scratch) = refs[:-4], refs[-4:]
+    total = jnp.zeros(scratch.shape, jnp.float32)
+    for k, answer in enumerate(answers):
         total += lax.dot_general(
             weigh[k],
             answer[...],
             (((0,), (0,)), ((), ())),
             preferred_element_type=jnp.float32,
         )
-    out[...] = total.astype(jnp.bfloat16)
+    scratch[...] = total
+    half = left.shape[1]
+    parity = lax.axis_index("zp")
+    pair = 2 * row_count
+    for i in range(keep.shape[0] // pair):
+        for mine in (True, False):
+            odd = parity if mine else 1 - parity
+            block = jnp.concatenate(
+                [
+                    scratch[pl.ds(pl.multiple_of((4 * i + j + odd) * row_count, 8), row_count), :]
+                    for j in (0, 2)
+                ],
+                axis=0,
+            )
+            rows = pl.ds(i * pair, pair)
+            if mine:
+                keep[rows, :] = block
+            else:
+                left[rows, :] = block[:, :half].astype(jnp.bfloat16)
+                right[rows, :] = block[:, half:].astype(jnp.bfloat16)
+
+
+def merge_body(keep, left, right, out):
+    half = left.shape[1]
+    out[:, :half] = (keep[:, :half] + left[...].astype(jnp.float32)).astype(jnp.bfloat16)
+    out[:, half:] = (keep[:, half:] + right[...].astype(jnp.float32)).astype(jnp.bfloat16)
 
 
 def layer(
@@ -222,7 +256,7 @@
         in_specs=[whole] * 4,
         out_specs=whole,
     )(hidden_states, norm_gain, expert_ids, route_scores)
-    gathered = lax.all_gather(packed, "z", axis=0, tiled=True)
+    gathered = lax.all_gather(packed, z_axes, axis=0, tiled=True)
 
     y_size = lax.axis_size("y")
     slots = gathered.shape[0] // row_count * MOST
@@ -260,23 +294,39 @@
         tree_parents,
     )
 
-    summed = pl.pallas_call(
-        expand_body,
-        out_shape=jax.ShapeDtypeStruct((gathered.shape[0], width), jnp.bfloat16),
+    held = gathered.shape[0] // 2
+    small = pltpu.CompilerParams(vmem_limit_bytes=16 << 20)
+    keep, left, right = pl.pallas_call(
+        functools.partial(expand_body, row_count),
+        out_shape=[
+            jax.ShapeDtypeStruct((held, width), jnp.float32),
+            jax.ShapeDtypeStruct((held, width // 2), jnp.bfloat16),
+            jax.ShapeDtypeStruct((held, width // 2), jnp.bfloat16),
+        ],
         in_specs=[whole] * (y_size + 1),
+        out_specs=[whole] * 3,
+        scratch_shapes=[pltpu.VMEM((2 * held, width), jnp.float32)],
+        compiler_params=small,
+    )(weigh, *returned)
+    left = shifted(left, z_axes, 1)
+    right = shifted(right, z_axes, -1)
+    merged = pl.pallas_call(
+        merge_body,
+        out_shape=jax.ShapeDtypeStruct((held, width), jnp.bfloat16),
+        in_specs=[whole] * 3,
         out_specs=whole,
-        compiler_params=pltpu.CompilerParams(vmem_limit_bytes=16 << 20),
-    )(weigh, *returned)
-    parts = lax.all_to_all(summed, "z", split_axis=0, concat_axis=0, tiled=True)
+        compiler_params=small,
+    )(keep, left, right)
+    parts = lax.all_to_all(merged, "zi", split_axis=0, concat_axis=0, tiled=True)
     expert_out = jnp.sum(parts.reshape(-1, row_count, width).astype(jnp.float32), axis=0)
     return (attention_out, expert_out.astype(jnp.bfloat16))
 
 
 def solution(mesh):
-    devices = mesh.devices.reshape(4, 4, 16, 2)
+    devices = mesh.devices.reshape(4, 4, 8, 2, 2)
     grid = Mesh(devices, grid_axes)
     rows = P(grid_axes, None)
-    ep = ("y", "z", "c")
+    ep = ("y", *z_axes, "c")
     placed = (
         rows,
         P(),

time: 180 us -> 175 us (0.972)
  the two profiles are of different devices: /device:TPU:38 before, /device:TPU:2 now
where the time goes in v2:
time: 175 us
  waiting for transfers between devices  73.6 us (42%)
  starting transfers between devices  41.4 us (24%)
  blocking collectives  41.3 us (24%)
  Pallas kernels  8.72 us (5%)
  matrix products  4.62 us (3%)
  local copies, waits for them, and re-layouts  2.25 us (1%)
    ppermute x11, waiting for transfers between devices, shifted(): lax.ppermute(value, axis, [(i, (i + step) % size) for i in range(size)])  50 us
    all_gather x1, blocking collectives, layer(): gathered = lax.all_gather(packed, z_axes, axis=0, tiled=True)  41.3 us
    ppermute x11, starting transfers between devices, shifted(): lax.ppermute(value, axis, [(i, (i + step) % size) for i in range(size)])  34 us
    all_to_all x1, waiting for transfers between devices, layer(): lax.all_to_all(merged, 'zi', split_axis=0, concat_axis=0, tiled=True)  23.5 us
    all_to_all x1, starting transfers between devices, layer(): lax.all_to_all(merged, 'zi', split_axis=0, concat_axis=0, tiled=True)  7.44 us
    pallas_call x1, Pallas kernels, expert_part(): pl.pallas_call(functools.partial(expert_body, len(rows)), out_shape=[jax....  3.79 us
  transfers between devices with their start and end apart: 12, of which 7 were waited for; matrix products, arithmetic and copies ran while one was open for 3% of the time, Pallas kernels for 0%

profile of v2, /device:TPU:2, one launch (start us, length us, event | category | flops | bytes accessed | tf_op | source)
XLA Modules:
  0.0 174.6 jit_solution(4303625821741877161)
XLA Ops:
  0.6 0.0 copy-start
  0.6 1.7 shard_map.158
  2.4 41.3 %all_gather.3.gathered = bf16[128,3712]{1,0:T(8,128)(2,1)S(1)} all-gather(bf16[8,3712]{1,0:T(8,128)(2,1)} %shard_map.158), channel_id=1, replica_groups=mesh['dp'=4,'y'=4,'zi'=8,'zp'=2,'c'=2] {'zi','zp'}, dimensions={0}, use_global_device_ids=true | all-gather | bytes 1009664 | tf_op jit(solution)/shard_map/all_gather | solution.py:259
  43.6 1.0 shard_map.159
  44.7 3.5 %collective-permute-start = (bf16[80,3584]{1,0:T(8,128)(2,1)S(1)}, bf16[80,3584]{1,0:T(8,128)(2,1)S(1)}, u32[]{:S(2)}, u32[]{:S(2)}) collective-permute-start(bf16[80,3584]{1,0:T(8,128)(2,1)S(1)} %get-tuple-element.27), channel_id=1, source_target_pairs={{0,32},{32,64},{64,96},{96,0},{1,33},{33,65},{65,97},{97,1},{2,34}... | collective-permute-start | bytes 1720328 | tf_op jit(solution)/shard_map/ppermute | solution.py:155
  48.2 1.9 %collective-permute-start.3 = (bf16[3584,128]{1,0:T(8,128)(2,1)S(1)}, bf16[3584,128]{1,0:T(8,128)(2,1)S(1)}, u32[]{:S(2)}, u32[]{:S(2)}) collective-permute-start(bf16[3584,128]{1,0:T(8,128)(2,1)S(1)} %copy-done.1), channel_id=1, source_target_pairs={{0,1},{1,0},{2,3},{3,2},{4,5},{5,4},{6,7},{7,6},{8,9},{9,8},{10,11... | collective-permute-start | bytes 2752520 | tf_op jit(solution)/shard_map/ppermute | solution.py:155
  50.1 2.4 %collective-permute-start.4 = (bf16[3584,128]{1,0:T(8,128)(2,1)S(1)}, bf16[3584,128]{1,0:T(8,128)(2,1)S(1)}, u32[]{:S(2)}, u32[]{:S(2)}) collective-permute-start(bf16[3584,128]{1,0:T(8,128)(2,1)S(1)} %copy-done.2), channel_id=1, source_target_pairs={{0,1},{1,0},{2,3},{3,2},{4,5},{5,4},{6,7},{7,6},{8,9},{9,8},{10,11... | collective-permute-start | bytes 2752520 | tf_op jit(solution)/shard_map/ppermute | solution.py:155
  52.5 1.9 %collective-permute-start.5 = (bf16[128,3584]{1,0:T(8,128)(2,1)}, bf16[128,3584]{1,0:T(8,128)(2,1)S(1)}, u32[]{:S(2)}, u32[]{:S(2)}) collective-permute-start(bf16[128,3584]{1,0:T(8,128)(2,1)} %refs_6_), channel_id=1, source_target_pairs={{0,1},{1,0},{2,3},{3,2},{4,5},{5,4},{6,7},{7,6},{8,9},{9,8},{10,11... | collective-permute-start | bytes 2752520 | tf_op jit(solution)/shard_map/ppermute | solution.py:155
  54.4 4.8 %collective-permute-start.1 = (bf16[80,3584]{1,0:T(8,128)(2,1)S(1)}, bf16[80,3584]{1,0:T(8,128)(2,1)S(1)}, u32[]{:S(2)}, u32[]{:S(2)}) collective-permute-start(bf16[80,3584]{1,0:T(8,128)(2,1)S(1)} %get-tuple-element.28), channel_id=1, source_target_pairs={{0,64},{32,96},{64,0},{96,32},{1,65},{33,97},{65,1},{97,33},{2,66}... | collective-permute-start | bytes 1720328 | tf_op jit(solution)/shard_map/ppermute | solution.py:155
  59.3 0.2 fusion.12
  59.5 0.2 fusion.11
  59.7 3.3 %collective-permute-start.2 = (bf16[80,3584]{1,0:T(8,128)(2,1)S(1)}, bf16[80,3584]{1,0:T(8,128)(2,1)S(1)}, u32[]{:S(2)}, u32[]{:S(2)}) collective-permute-start(bf16[80,3584]{1,0:T(8,128)(2,1)S(1)} %get-tuple-element.29), channel_id=1, source_target_pairs={{0,96},{32,0},{64,32},{96,64},{1,97},{33,1},{65,33},{97,65},{2,98}... | collective-permute-start | bytes 1720328 | tf_op jit(solution)/shard_map/ppermute | solution.py:155
  62.9 0.2 fusion.10
  63.1 0.2 fusion.9
  63.3 0.2 fusion.8
  63.5 9.7 %collective-permute-done.1.refs_2_ = bf16[80,3584]{1,0:T(8,128)(2,1)S(1)} collective-permute-done((bf16[80,3584]{1,0:T(8,128)(2,1)S(1)}, bf16[80,3584]{1,0:T(8,128)(2,1)S(1)}, u32[]{:S(2)}, u32[]{:S(2)}) %collective-permute-start.1) | collective-permute-done | bytes 573472 | tf_op jit(solution)/shard_map/ppermute | solution.py:155
  73.2 11.3 %collective-permute-done.2.refs_3_ = bf16[80,3584]{1,0:T(8,128)(2,1)S(1)} collective-permute-done((bf16[80,3584]{1,0:T(8,128)(2,1)S(1)}, bf16[80,3584]{1,0:T(8,128)(2,1)S(1)}, u32[]{:S(2)}, u32[]{:S(2)}) %collective-permute-start.2) | collective-permute-done | bytes 573472 | tf_op jit(solution)/shard_map/ppermute | solution.py:155
  84.6 1.2 copy-done.3
  85.7 3.8 %shard_map.160 = (bf16[80,3584]{1,0:T(8,128)(2,1)S(1)}, bf16[80,3584]{1,0:T(8,128)(2,1)S(1)}, bf16[80,3584]{1,0:T(8,128)(2,1)S(1)}, bf16[80,3584]{1,0:T(8,128)(2,1)S(1)}) custom-call(bf16[80,3584]{1,0:T(8,128)(2,1)S(1)} %get-tuple-element.26.refs_0_, bf16[80,3584]{1,0:T(8,128)(2,1)S(1)} %collective-permute-done.refs_1_, ...), custom_call_target="tpu_custom_call" | custom-call | flops 1761607680 | bytes 10092544 | tf_op jit(solution)/shard_map/pallas_call | solution.py:182
  89.5 4.5 %collective-permute-start.6 = (bf16[80,3584]{1,0:T(8,128)(2,1)S(1)}, bf16[80,3584]{1,0:T(8,128)(2,1)S(1)}, u32[]{:S(2)}, u32[]{:S(2)}) collective-permute-start(bf16[80,3584]{1,0:T(8,128)(2,1)S(1)} %get-tuple-element.34), channel_id=1, source_target_pairs={{0,96},{32,0},{64,32},{96,64},{1,97},{33,1},{65,33},{97,65},{2,98}... | collective-permute-start | bytes 1720328 | tf_op jit(solution)/shard_map/ppermute | solution.py:155
  94.1 3.9 %collective-permute-start.7 = (bf16[80,3584]{1,0:T(8,128)(2,1)S(1)}, bf16[80,3584]{1,0:T(8,128)(2,1)S(1)}, u32[]{:S(2)}, u32[]{:S(2)}) collective-permute-start(bf16[80,3584]{1,0:T(8,128)(2,1)S(1)} %get-tuple-element.35), channel_id=1, source_target_pairs={{0,64},{32,96},{64,0},{96,32},{1,65},{33,97},{65,1},{97,33},{2,66}... | collective-permute-start | bytes 1720328 | tf_op jit(solution)/shard_map/ppermute | solution.py:155
  98.0 1.9 %collective-permute-start.8 = (bf16[80,3584]{1,0:T(8,128)(2,1)S(1)}, bf16[80,3584]{1,0:T(8,128)(2,1)S(1)}, u32[]{:S(2)}, u32[]{:S(2)}) collective-permute-start(bf16[80,3584]{1,0:T(8,128)(2,1)S(1)} %get-tuple-element.36), channel_id=1, source_target_pairs={{0,32},{32,64},{64,96},{96,0},{1,33},{33,65},{65,97},{97,1},{2,34}... | collective-permute-start | bytes 1720328 | tf_op jit(solution)/shard_map/ppermute | solution.py:155
  99.9 0.2 fusion.7
  100.8 0.0 copy-start.7
  100.8 0.2 fusion.6
  101.0 0.5 copy-done.7
  101.5 0.3 fusion.29
  101.8 17.1 %collective-permute-done.6.refs_1_ = bf16[80,3584]{1,0:T(8,128)(2,1)S(1)} collective-permute-done((bf16[80,3584]{1,0:T(8,128)(2,1)S(1)}, bf16[80,3584]{1,0:T(8,128)(2,1)S(1)}, u32[]{:S(2)}, u32[]{:S(2)}) %collective-permute-start.6) | collective-permute-done | bytes 573472 | tf_op jit(solution)/shard_map/ppermute | solution.py:155
  118.8 5.6 %collective-permute-done.8.refs_3_ = bf16[80,3584]{1,0:T(8,128)(2,1)S(1)} collective-permute-done((bf16[80,3584]{1,0:T(8,128)(2,1)S(1)}, bf16[80,3584]{1,0:T(8,128)(2,1)S(1)}, u32[]{:S(2)}, u32[]{:S(2)}) %collective-permute-start.8) | collective-permute-done | bytes 573472 | tf_op jit(solution)/shard_map/ppermute | solution.py:155
  124.4 1.3 shard_map.161
  125.8 1.9 %collective-permute-start.10 = (bf16[64,1792]{1,0:T(8,128)(2,1)S(1)}, bf16[64,1792]{1,0:T(8,128)(2,1)S(1)}, u32[]{:S(2)}, u32[]{:S(2)}) collective-permute-start(bf16[64,1792]{1,0:T(8,128)(2,1)S(1)} %get-tuple-element.39), channel_id=1, source_target_pairs={{0,30},{2,0},{4,2},{6,4},{8,6},{10,8},{12,10},{14,12},{16,14},{18,... | collective-permute-start | bytes 688136 | tf_op jit(solution)/shard_map/ppermute | solution.py:155
  127.7 3.9 %collective-permute-start.9 = (bf16[64,1792]{1,0:T(8,128)(2,1)S(1)}, bf16[64,1792]{1,0:T(8,128)(2,1)S(1)}, u32[]{:S(2)}, u32[]{:S(2)}) collective-permute-start(bf16[64,1792]{1,0:T(8,128)(2,1)S(1)} %get-tuple-element.38), channel_id=1, source_target_pairs={{0,2},{2,4},{4,6},{6,8},{8,10},{10,12},{12,14},{14,16},{16,18},{18... | collective-permute-start | bytes 688136 | tf_op jit(solution)/shard_map/ppermute | solution.py:155
  131.7 0.2 reshape.34
  131.8 0.2 fusion.13
  132.0 3.2 %collective-permute-done.10.right = bf16[64,1792]{1,0:T(8,128)(2,1)S(1)} collective-permute-done((bf16[64,1792]{1,0:T(8,128)(2,1)S(1)}, bf16[64,1792]{1,0:T(8,128)(2,1)S(1)}, u32[]{:S(2)}, u32[]{:S(2)}) %collective-permute-start.10) | collective-permute-done | bytes 229408 | tf_op jit(solution)/shard_map/ppermute | solution.py:155
  135.2 3.1 %collective-permute-done.9.left = bf16[64,1792]{1,0:T(8,128)(2,1)S(1)} collective-permute-done((bf16[64,1792]{1,0:T(8,128)(2,1)S(1)}, bf16[64,1792]{1,0:T(8,128)(2,1)S(1)}, u32[]{:S(2)}, u32[]{:S(2)}) %collective-permute-start.9) | collective-permute-done | bytes 229408 | tf_op jit(solution)/shard_map/ppermute | solution.py:155
  138.3 0.9 shard_map.162
  139.2 7.4 %all-to-all-start = ((bf16[8,8,3584]{2,1,0:T(8,128)(2,1)}), bf16[8,8,3584]{2,1,0:T(8,128)(2,1)S(1)}, u32[]{:S(2)}, u32[]{:S(2)}) async-start(bf16[8,8,3584]{2,1,0:T(8,128)(2,1)} %bitcast.7), calls=%async_computation | async-start | bytes 917504 | tf_op jit(solution)/shard_map/all_to_all | solution.py:320
  146.6 0.2 fusion.60
  146.9 0.5 fusion.17
  147.4 0.4 copy-done.6
  147.7 0.4 fusion.59
  148.1 0.1 fusion.23
  148.2 0.3 fusion.14
  148.6 0.5 fusion.15
  149.1 1.2 fusion.2
  150.3 23.5 %all-to-all-done = bf16[8,8,3584]{2,1,0:T(8,128)(2,1)S(1)} async-done(((bf16[8,8,3584]{2,1,0:T(8,128)(2,1)}), bf16[8,8,3584]{2,1,0:T(8,128)(2,1)S(1)}, u32[]{:S(2)}, u32[]{:S(2)}) %all-to-all-start) | async-done | bytes 458784 | tf_op jit(solution)/shard_map/all_to_all | solution.py:320
  173.9 0.7 reduce_sum.32
  (24 shorter events, 0.1 us)
Async XLA Ops:
  0.6 146.3 %copy-start = (bf16[1,512,512]{2,1,0:T(8,128)(2,1)S(1)}, bf16[1,512,512]{2,1,0:T(8,128)(2,1)}, u32[]{:S(2)}) copy-start(bf16[1,512,512]{2,1,0:T(8,128)(2,1)} %param.24) | copy-start | bytes 1572868
  2.4 45.8 %copy-start.1 = (bf16[3584,128]{1,0:T(8,128)(2,1)S(1)}, bf16[3584,128]{1,0:T(8,128)(2,1)}, u32[]{:S(2)}) copy-start(bf16[3584,128]{1,0:T(8,128)(2,1)} %refs_4_) | copy-start | bytes 2752516
  2.4 47.7 %copy-start.2 = (bf16[3584,128]{1,0:T(8,128)(2,1)S(1)}, bf16[3584,128]{1,0:T(8,128)(2,1)}, u32[]{:S(2)}) copy-start(bf16[3584,128]{1,0:T(8,128)(2,1)} %refs_5_) | copy-start | bytes 2752516
  44.6 14.6 %copy-start.9 = (s32[8]{0:T(128)S(1)}, s32[8]{0:T(128)}, u32[]{:S(2)}) copy-start(s32[8]{0:T(128)} %param.29) | copy-start | bytes 100
  44.7 15.0 %collective-permute-start = (bf16[80,3584]{1,0:T(8,128)(2,1)S(1)}, bf16[80,3584]{1,0:T(8,128)(2,1)S(1)}, u32[]{:S(2)}, u32[]{:S(2)}) collective-permute-start(bf16[80,3584]{1,0:T(8,128)(2,1)S(1)} %get-tuple-element.27), channel_id=1, source_target_pairs={{0,32},{32,64},{64,96},{96,0},{1,33},{33,65},{65,97},{97,1},{2,34}... | collective-permute-start | bytes 1720328 | tf_op jit(solution)/shard_map/ppermute | solution.py:155
  48.2 36.4 %collective-permute-start.3 = (bf16[3584,128]{1,0:T(8,128)(2,1)S(1)}, bf16[3584,128]{1,0:T(8,128)(2,1)S(1)}, u32[]{:S(2)}, u32[]{:S(2)}) collective-permute-start(bf16[3584,128]{1,0:T(8,128)(2,1)S(1)} %copy-done.1), channel_id=1, source_target_pairs={{0,1},{1,0},{2,3},{3,2},{4,5},{5,4},{6,7},{7,6},{8,9},{9,8},{10,11... | collective-permute-start | bytes 2752520 | tf_op jit(solution)/shard_map/ppermute | solution.py:155
  50.1 34.5 %collective-permute-start.4 = (bf16[3584,128]{1,0:T(8,128)(2,1)S(1)}, bf16[3584,128]{1,0:T(8,128)(2,1)S(1)}, u32[]{:S(2)}, u32[]{:S(2)}) collective-permute-start(bf16[3584,128]{1,0:T(8,128)(2,1)S(1)} %copy-done.2), channel_id=1, source_target_pairs={{0,1},{1,0},{2,3},{3,2},{4,5},{5,4},{6,7},{7,6},{8,9},{9,8},{10,11... | collective-permute-start | bytes 2752520 | tf_op jit(solution)/shard_map/ppermute | solution.py:155
  52.5 32.0 %collective-permute-start.5 = (bf16[128,3584]{1,0:T(8,128)(2,1)}, bf16[128,3584]{1,0:T(8,128)(2,1)S(1)}, u32[]{:S(2)}, u32[]{:S(2)}) collective-permute-start(bf16[128,3584]{1,0:T(8,128)(2,1)} %refs_6_), channel_id=1, source_target_pairs={{0,1},{1,0},{2,3},{3,2},{4,5},{5,4},{6,7},{7,6},{8,9},{9,8},{10,11... | collective-permute-start | bytes 2752520 | tf_op jit(solution)/shard_map/ppermute | solution.py:155
  54.4 18.8 %collective-permute-start.1 = (bf16[80,3584]{1,0:T(8,128)(2,1)S(1)}, bf16[80,3584]{1,0:T(8,128)(2,1)S(1)}, u32[]{:S(2)}, u32[]{:S(2)}) collective-permute-start(bf16[80,3584]{1,0:T(8,128)(2,1)S(1)} %get-tuple-element.28), channel_id=1, source_target_pairs={{0,64},{32,96},{64,0},{96,32},{1,65},{33,97},{65,1},{97,33},{2,66}... | collective-permute-start | bytes 1720328 | tf_op jit(solution)/shard_map/ppermute | solution.py:155
  59.7 24.9 %collective-permute-start.2 = (bf16[80,3584]{1,0:T(8,128)(2,1)S(1)}, bf16[80,3584]{1,0:T(8,128)(2,1)S(1)}, u32[]{:S(2)}, u32[]{:S(2)}) collective-permute-start(bf16[80,3584]{1,0:T(8,128)(2,1)S(1)} %get-tuple-element.29), channel_id=1, source_target_pairs={{0,96},{32,0},{64,32},{96,64},{1,97},{33,1},{65,33},{97,65},{2,98}... | collective-permute-start | bytes 1720328 | tf_op jit(solution)/shard_map/ppermute | solution.py:155
  84.6 1.2 copy-start.3
  85.7 15.2 %copy-start.4 = (bf16[8,64,512]{2,1,0:T(8,128)(2,1)S(1)}, bf16[8,64,512]{2,1,0:T(8,128)(2,1)}, u32[]{:S(2)}) copy-start(bf16[8,64,512]{2,1,0:T(8,128)(2,1)} %param.22) | copy-start | bytes 1572868
  89.5 29.3 %collective-permute-start.6 = (bf16[80,3584]{1,0:T(8,128)(2,1)S(1)}, bf16[80,3584]{1,0:T(8,128)(2,1)S(1)}, u32[]{:S(2)}, u32[]{:S(2)}) collective-permute-start(bf16[80,3584]{1,0:T(8,128)(2,1)S(1)} %get-tuple-element.34), channel_id=1, source_target_pairs={{0,96},{32,0},{64,32},{96,64},{1,97},{33,1},{65,33},{97,65},{2,98}... | collective-permute-start | bytes 1720328 | tf_op jit(solution)/shard_map/ppermute | solution.py:155
  94.1 24.7 %collective-permute-start.7 = (bf16[80,3584]{1,0:T(8,128)(2,1)S(1)}, bf16[80,3584]{1,0:T(8,128)(2,1)S(1)}, u32[]{:S(2)}, u32[]{:S(2)}) collective-permute-start(bf16[80,3584]{1,0:T(8,128)(2,1)S(1)} %get-tuple-element.35), channel_id=1, source_target_pairs={{0,64},{32,96},{64,0},{96,32},{1,65},{33,97},{65,1},{97,33},{2,66}... | collective-permute-start | bytes 1720328 | tf_op jit(solution)/shard_map/ppermute | solution.py:155
  98.0 26.4 %collective-permute-start.8 = (bf16[80,3584]{1,0:T(8,128)(2,1)S(1)}, bf16[80,3584]{1,0:T(8,128)(2,1)S(1)}, u32[]{:S(2)}, u32[]{:S(2)}) collective-permute-start(bf16[80,3584]{1,0:T(8,128)(2,1)S(1)} %get-tuple-element.36), channel_id=1, source_target_pairs={{0,32},{32,64},{64,96},{96,0},{1,33},{33,65},{65,97},{97,1},{2,34}... | collective-permute-start | bytes 1720328 | tf_op jit(solution)/shard_map/ppermute | solution.py:155
  100.8 0.7 copy-start.7
  124.4 7.2 %copy-start.5 = (bf16[8,4096]{1,0:T(8,128)(2,1)S(1)}, bf16[8,4096]{1,0:T(8,128)(2,1)}, u32[]{:S(2)}) copy-start(bf16[8,4096]{1,0:T(8,128)(2,1)} %param.23) | copy-start | bytes 196612
  125.8 9.4 %collective-permute-start.10 = (bf16[64,1792]{1,0:T(8,128)(2,1)S(1)}, bf16[64,1792]{1,0:T(8,128)(2,1)S(1)}, u32[]{:S(2)}, u32[]{:S(2)}) collective-permute-start(bf16[64,1792]{1,0:T(8,128)(2,1)S(1)} %get-tuple-element.39), channel_id=1, source_target_pairs={{0,30},{2,0},{4,2},{6,4},{8,6},{10,8},{12,10},{14,12},{16,14},{18,... | collective-permute-start | bytes 688136 | tf_op jit(solution)/shard_map/ppermute | solution.py:155
  127.7 10.6 %collective-permute-start.9 = (bf16[64,1792]{1,0:T(8,128)(2,1)S(1)}, bf16[64,1792]{1,0:T(8,128)(2,1)S(1)}, u32[]{:S(2)}, u32[]{:S(2)}) collective-permute-start(bf16[64,1792]{1,0:T(8,128)(2,1)S(1)} %get-tuple-element.38), channel_id=1, source_target_pairs={{0,2},{2,4},{4,6},{6,8},{8,10},{10,12},{12,14},{14,16},{16,18},{18... | collective-permute-start | bytes 688136 | tf_op jit(solution)/shard_map/ppermute | solution.py:155
  139.2 7.4 %copy-start.8 = (bf16[8,64]{1,0:T(8,128)(2,1)S(1)}, bf16[8,64]{1,0:T(8,128)(2,1)}, u32[]{:S(2)}) copy-start(bf16[8,64]{1,0:T(8,128)(2,1)} %param.27) | copy-start | bytes 3076
  139.2 34.7 %all-to-all-start = ((bf16[8,8,3584]{2,1,0:T(8,128)(2,1)}), bf16[8,8,3584]{2,1,0:T(8,128)(2,1)S(1)}, u32[]{:S(2)}, u32[]{:S(2)}) async-start(bf16[8,8,3584]{2,1,0:T(8,128)(2,1)} %bitcast.7), calls=%async_computation | async-start | bytes 917504 | tf_op jit(solution)/shard_map/all_to_all | solution.py:320
  146.9 0.8 copy-start.6
